TPU v7x, 128 devices: a whole 4x4x4 slice. The times are simulated.
128 devices in a mesh: row: 16 (over y_lo, x, core), col: 8 (over y_hi, z).
Axes of the slice: x: 4, y: 4 (y_hi: 2, y_lo: 2; y = y_hi * 2 + y_lo), z: 4, core: 2. Of those that a mesh axis runs over, the one named last changes fastest.
Arguments:
- cholesky_vectors: float32 [256, 512, 512], P(('row', 'col')), as said below
- factor: float32 [512, 2048], P(('row', 'col')), may hold values from -0.25 to 0.25
- core_weights: float32 [256, 2048], P(('row', 'col')), may hold values from -0.375 to 0.375
Outputs:
- core_gradient: float32 [256, 2048], P(('row', 'col'))
- factor_gradient: float32 [512, 2048], P('row', 'col')
Inputs may be any that keep to these rules, and one draw needn't show every extreme that they name: Each cholesky_vectors[P] is symmetric.
All inputs are finite; a program needn't handle non-finite values.
Results may differ from a plain program's by a relative error of at most 0.0001.
Values sent between devices are 32-bit elements; how exact they have to be, the bound alone decides.
A program may use at most 384 MiB of HBM per device.

v0:
```python
import jax
import jax.numpy as jnp
from jax import lax
from jax.sharding import PartitionSpec as P

AXES = ("row", "col")


def on_device(cholesky_vectors, factor, core_weights):
    high = lax.Precision.HIGHEST
    rank = factor.shape[1]
    rows, cols = (lax.axis_size("row"), lax.axis_size("col"))
    r, c = (lax.axis_index("row"), lax.axis_index("col"))
    x = lax.all_gather(factor, AXES, axis=0, tiled=True)
    z = lax.all_gather(core_weights, AXES, axis=0, tiled=True)
    orbitals, width = (x.shape[0], rank // cols)

    def dot(a, b, dims):
        return lax.dot_general(
            a, b, (dims, ((), ())), precision=high, preferred_element_type=jnp.float32
        )

    adjoint = jnp.einsum(
        "pab,bc->pac", cholesky_vectors, x, precision=high, preferred_element_type=jnp.float32
    )
    projection = jnp.sum(x[None] * adjoint, axis=1)
    part = jnp.sum(adjoint * core_weights[:, None, :], axis=0)
    part = part.reshape(rows, orbitals // rows, cols, width).transpose(0, 2, 1, 3)
    part = part.reshape(rows * cols, orbitals // rows, width)
    summed = lax.psum_scatter(part, AXES, scatter_dimension=0, tiled=True)[0]
    x_c = lax.dynamic_slice_in_dim(x, c * width, width, 1)
    z_c = lax.dynamic_slice_in_dim(z, c * width, width, 1)
    gram = dot(x_c, x, ((0,), (0,)))
    core_gram = dot(z_c, z, ((0,), (0,)))
    x_r = lax.dynamic_slice_in_dim(x, r * (orbitals // rows), orbitals // rows, 0)
    z_r = lax.dynamic_slice_in_dim(z, r * (z.shape[0] // rows), z.shape[0] // rows, 0)
    first = dot(x_r, gram * core_gram, ((1,), (1,)))
    weighted = dot(z_r, gram * gram, ((1,), (1,)))
    own = lax.all_to_all(weighted, "col", split_axis=0, concat_axis=1, tiled=True)
    return (own - projection, 4.0 * (first - summed))


def solution(mesh):
    placed = (P(AXES, None, None), P(AXES, None), P(AXES, None))
    return jax.shard_map(
        on_device,
        mesh=mesh,
        in_specs=placed,
        out_specs=(P(AXES, None), P("row", "col")),
        check_vma=False,
    )
```

profile of v0, /device:TPU:0, one launch (start us, length us, event | category | flops | bytes accessed | tf_op | source)
XLA Modules:
  0.0 1287.9 jit_solution(15794297128244354943)
XLA Ops:
  7.2 0.0 all-gather.7.cloned.1.call-start
  7.2 0.7 all-gather.7.cloned.1.call-update
  7.9 0.0 all-gather.5.cloned.1.call-start
  8.0 0.7 all-gather.5.cloned.1.call-update
  8.7 0.0 reduce-scatter.2.cloned.1.call-start
  8.7 307.2 %all-gather.7.cloned.1.call-done = f32[128,4,2048]{2,1,0:T(4,128)} async-done(((f32[1,4,2048]{2,1,0:T(4,128)}), f32[128,4,2048]{2,1,0:T(4,128)}) %all-gather.7.cloned.1.call-update) | async-done | bytes 4194320 | tf_op jit(solution)/shard_map/all_gather | solution.py:14
  315.9 5.3 reshape.20
  321.2 5.3 reshape.21
  326.5 17.0 %multiply_reduce_fusion = (f32[512,2048]{1,0:T(8,128)S(1)}, f32[2,2048]{1,0:T(2,128)S(1)}) fusion(f32[2,2048]{1,0:T(2,128)S(1)} %copy-done.2, f32[512,2048]{1,0:T(8,128)} %reshape.20, f32[2,512,512]{2,1,0:T(8,128)S(1)} %copy-done, f32[512,2048,1]{1,0,2:T(8,128)} %reshape.21), kind=kOutput, calls=%fused_computation | convolution fusion | flops 12892237824 | bytes 14712832 | tf_op jit(solution)/shard_map/pab,bc->pac/dot_general | solution.py:23
  343.6 2.0 copy.10
  345.5 0.4 bitcast_bitcast_fusion
  345.9 3.3 copy.9
  349.2 272.3 %all-gather.5.cloned.1.call-done = f32[128,2,2048]{2,1,0:T(2,128)} async-done(((f32[1,2,2048]{2,1,0:T(2,128)}), f32[128,2,2048]{2,1,0:T(2,128)}) %all-gather.5.cloned.1.call-update) | async-done | bytes 2097168 | tf_op jit(solution)/shard_map/all_gather | solution.py:15
  621.5 3.7 reshape.18
  625.2 5.5 fusion.3
  630.7 1.3 copy-done.1
  632.0 2.6 fusion
  634.6 0.6 all_to_all.14
  635.3 6.7 all-to-all-start
  642.0 5.6 convolution_multiply_fusion
  647.6 2.2 all-to-all-done
  649.7 0.6 sub.6
  650.3 626.9 %reduce-scatter.2.cloned.1.call-done = f32[1,32,256]{2,1,0:T(8,128)} async-done(((f32[128,32,256]{2,1,0:T(8,128)}), f32[1,32,256]{2,1,0:T(8,128)}) %reduce-scatter.2.cloned.1.call-update) | async-done | bytes 32784 | tf_op jit(solution)/shard_map/reduce_scatter | solution.py:30
  1277.3 4.1 fusion.2
  (6 shorter events, 0.0 us)
Async XLA Ops:
  7.2 319.4 %copy-start = (f32[2,512,512]{2,1,0:T(8,128)S(1)}, f32[2,512,512]{2,1,0:T(8,128)}, u32[]{:S(2)}) copy-start(f32[2,512,512]{2,1,0:T(8,128)} %param.3) | copy-start | bytes 6291460
  7.2 308.7 %all-gather.7.cloned.1.call-start = ((), (), s32[]{:S(2)}) async-start(), calls=%async_computation.4 | async-start | bytes 4227072 | tf_op jit(solution)/shard_map/all_gather | solution.py:14
  7.9 613.6 %all-gather.5.cloned.1.call-start = ((), (), s32[]{:S(2)}) async-start(), calls=%async_computation.3 | async-start | bytes 2113536 | tf_op jit(solution)/shard_map/all_gather | solution.py:15
  8.7 1268.6 %reduce-scatter.2.cloned.1.call-start = ((), (), s32[]{:S(2)}) async-start(), calls=%async_computation.2 | async-start | bytes 4227072 | tf_op jit(solution)/shard_map/reduce_scatter | solution.py:30
  321.2 5.3 copy-start.2
  630.7 1.3 copy-start.1
  635.3 14.4 %all-to-all-start = ((f32[8,2,256]{2,1,0:T(2,128)}), f32[8,2,256]{2,1,0:T(2,128)S(1)}, u32[]{:S(2)}, u32[]{:S(2)}) async-start(f32[8,2,256]{2,1,0:T(2,128)} %all_to_all.14), calls=%async_computation | async-start | bytes 32768 | tf_op jit(solution)/shard_map/all_to_all | solution.py:39
Sparse Core Ops, SparseCore 0:
  9.7 306.1 all-gather.6
  317.6 303.8 all-gather.4
  623.9 653.3 reduce-scatter.1
where the time goes:
time: 1290 us
  waiting for transfers between devices  1210 us (94%)
  matrix products  34.8 us (3%)
  local copies, waits for them, and re-layouts  21.9 us (2%)
  between operations  13.8 us (1%)
    reduce_scatter x1, waiting for transfers between devices, on_device(): summed = lax.psum_scatter(part, AXES, scatter_dimension=0, tiled=True)[0]  627 us
    all_gather x1, waiting for transfers between devices, on_device(): x = lax.all_gather(factor, AXES, axis=0, tiled=True)  307 us
    all_gather x1, waiting for transfers between devices, on_device(): z = lax.all_gather(core_weights, AXES, axis=0, tiled=True)  272 us
  transfers between devices with their start and end apart: 4, of which 4 were waited for; matrix products, arithmetic and copies ran while one was open for 4% of the time, Pallas kernels for 0%

commit v1 on v0

--- a/solution.py
+++ b/solution.py
@@ -11,7 +11,9 @@
     rank = factor.shape[1]
     rows, cols = (lax.axis_size("row"), lax.axis_size("col"))
     r, c = (lax.axis_index("row"), lax.axis_index("col"))
-    x = lax.all_gather(factor, AXES, axis=0, tiled=True)
+    x = jnp.concatenate(
+        lax.all_to_all(jnp.stack([factor] * lax.axis_size(AXES)), AXES, 0, 0), axis=0
+    )
     z = lax.all_gather(core_weights, AXES, axis=0, tiled=True)
     orbitals, width = (x.shape[0], rank // cols)
 

time: 1290 us -> 1010 us (0.78)
  waiting for transfers between devices: 1210 us -> 915 us
    all_gather x1 -> x0, waiting for transfers between devices: 307 us -> none  [on_device(): x = lax.all_gather(factor, AXES, axis=0, tiled=True)]
    all_to_all x0 -> x1, waiting for transfers between devices: none -> 51 us  [on_device(): lax.all_to_all(jnp.stack([factor] * lax.axis_size(AXES)), AXES, 0, 0)]
    all_gather x1, waiting for transfers between devices: 272 us -> 238 us  [on_device(): z = lax.all_gather(core_weights, AXES, axis=0, tiled=True)]
  transfers between devices with their start and end apart: 4 -> 4, of which waited for: 4 -> 4; matrix products, arithmetic and copies ran while one was open for 4% -> 5% of each run, Pallas kernels for 0% -> 0%
where the time goes in v1:
time: 1010 us
  waiting for transfers between devices  915 us (91%)
  matrix products  34.8 us (3%)
  local copies, waits for them, and re-layouts  25.8 us (3%)
  starting transfers between devices  18.9 us (2%)
  between operations  14.1 us (1%)
    reduce_scatter x1, waiting for transfers between devices, on_device(): summed = lax.psum_scatter(part, AXES, scatter_dimension=0, tiled=True)[0]  623 us
    all_gather x1, waiting for transfers between devices, on_device(): z = lax.all_gather(core_weights, AXES, axis=0, tiled=True)  238 us
    all_to_all x1, waiting for transfers between devices, on_device(): lax.all_to_all(jnp.stack([factor] * lax.axis_size(AXES)), AXES, 0, 0)  51 us
  transfers between devices with their start and end apart: 4, of which 4 were waited for; matrix products, arithmetic and copies ran while one was open for 5% of the time, Pallas kernels for 0%

profile of v1, /device:TPU:0, one launch (start us, length us, event | category | flops | bytes accessed | tf_op | source)
XLA Modules:
  0.0 1009.2 jit_solution(10196879692168396115)
XLA Ops:
  7.2 3.9 stack.2
  11.1 11.7 %all-to-all-start = ((f32[128,4,2048]{2,1,0:T(4,128)}), f32[128,4,2048]{2,1,0:T(4,128)}, u32[]{:S(2)}, u32[]{:S(2)}) async-start(f32[128,4,2048]{2,1,0:T(4,128)} %stack.2), calls=%async_computation | async-start | bytes 8388608 | tf_op jit(solution)/shard_map/all_to_all | solution.py:15
  22.8 0.0 all-gather.3.cloned.1.call-start
  22.8 0.7 all-gather.3.cloned.1.call-update
  23.5 0.0 reduce-scatter.2.cloned.1.call-start
  23.6 51.0 %all-to-all-done = f32[128,4,2048]{2,1,0:T(4,128)} async-done(((f32[128,4,2048]{2,1,0:T(4,128)}), f32[128,4,2048]{2,1,0:T(4,128)}, u32[]{:S(2)}, u32[]{:S(2)}) %all-to-all-start) | async-done | bytes 4194336 | tf_op jit(solution)/shard_map/all_to_all | solution.py:15
  74.6 5.3 reshape.20
  79.8 5.3 reshape.25
  85.2 17.0 %multiply_reduce_fusion = (f32[512,2048]{1,0:T(8,128)S(1)}, f32[2,2048]{1,0:T(2,128)S(1)}) fusion(f32[2,2048]{1,0:T(2,128)S(1)} %copy-done.2, f32[512,2048]{1,0:T(8,128)} %reshape.20, f32[2,512,512]{2,1,0:T(8,128)S(1)} %copy-done, f32[512,2048,1]{1,0,2:T(8,128)} %reshape.25), kind=kOutput, calls=%fused_computation | convolution fusion | flops 12892237824 | bytes 14712832 | tf_op jit(solution)/shard_map/pab,bc->pac/dot_general | solution.py:25
  102.2 2.0 copy.10
  104.2 0.4 bitcast_bitcast_fusion
  104.6 3.3 copy.9
  107.9 238.4 %all-gather.3.cloned.1.call-done = f32[128,2,2048]{2,1,0:T(2,128)} async-done(((f32[1,2,2048]{2,1,0:T(2,128)}), f32[128,2,2048]{2,1,0:T(2,128)}) %all-gather.3.cloned.1.call-update) | async-done | bytes 2097168 | tf_op jit(solution)/shard_map/all_gather | solution.py:17
  346.3 3.7 reshape.24
  349.9 5.5 fusion.3
  355.4 1.3 copy-done.1
  356.7 2.6 fusion
  359.4 0.6 all_to_all.18
  360.0 7.1 all-to-all-start.1
  367.2 5.6 convolution_multiply_fusion
  372.7 2.2 all-to-all-done.1
  374.9 0.6 sub.6
  375.5 622.7 %reduce-scatter.2.cloned.1.call-done = f32[1,32,256]{2,1,0:T(8,128)} async-done(((f32[128,32,256]{2,1,0:T(8,128)}), f32[1,32,256]{2,1,0:T(8,128)}) %reduce-scatter.2.cloned.1.call-update) | async-done | bytes 32784 | tf_op jit(solution)/shard_map/reduce_scatter | solution.py:32
  998.2 4.1 fusion.2
  (6 shorter events, 0.0 us)
Async XLA Ops:
  7.2 78.0 %copy-start = (f32[2,512,512]{2,1,0:T(8,128)S(1)}, f32[2,512,512]{2,1,0:T(8,128)}, u32[]{:S(2)}) copy-start(f32[2,512,512]{2,1,0:T(8,128)} %param.3) | copy-start | bytes 6291460
  11.1 63.5 %all-to-all-start = ((f32[128,4,2048]{2,1,0:T(4,128)}), f32[128,4,2048]{2,1,0:T(4,128)}, u32[]{:S(2)}, u32[]{:S(2)}) async-start(f32[128,4,2048]{2,1,0:T(4,128)} %stack.2), calls=%async_computation | async-start | bytes 8388608 | tf_op jit(solution)/shard_map/all_to_all | solution.py:15
  22.8 323.5 %all-gather.3.cloned.1.call-start = ((), (), s32[]{:S(2)}) async-start(), calls=%async_computation.4 | async-start | bytes 2113536 | tf_op jit(solution)/shard_map/all_gather | solution.py:17
  23.5 974.7 %reduce-scatter.2.cloned.1.call-start = ((), (), s32[]{:S(2)}) async-start(), calls=%async_computation.3 | async-start | bytes 4227072 | tf_op jit(solution)/shard_map/reduce_scatter | solution.py:32
  79.8 5.3 copy-start.2
  355.4 1.3 copy-start.1
  360.0 14.9 %all-to-all-start.1 = ((f32[8,2,256]{2,1,0:T(2,128)}), f32[8,2,256]{2,1,0:T(2,128)S(1)}, u32[]{:S(2)}, u32[]{:S(2)}) async-start(f32[8,2,256]{2,1,0:T(2,128)} %all_to_all.18), calls=%async_computation.1 | async-start | bytes 32768 | tf_op jit(solution)/shard_map/all_to_all | solution.py:41
Sparse Core Ops, SparseCore 0:
  25.3 320.9 all-gather.2
  348.6 649.5 reduce-scatter.1
